TPU v7x, 256 devices: a whole 4x4x8 slice. The times are simulated.
256 devices in a mesh: dp: 4 (over y_lo, core), tm: 4 (over x), rows: 16 (over z, y_hi).
Axes of the slice: x: 4, y: 4 (y_hi: 2, y_lo: 2; y = y_hi * 2 + y_lo), z: 8, core: 2. Of those that a mesh axis runs over, the one named last changes fastest.
Arguments:
- latents: bfloat16 [4, 8, 16, 30, 512], P('dp', 'tm', 'rows'), may hold values from -6 to 6
- grad_out: bfloat16 [4, 8, 32, 60, 256], P('dp', 'tm', 'rows'), may hold values from -6 to 6
- kernel: bfloat16 [3, 3, 3, 512, 256], replicated, may hold values from -0.0546875 to 0.0546875
Outputs:
- grad_latents: bfloat16 [4, 8, 16, 30, 512], P('dp', 'tm', 'rows')
- weight_grad: float32 [512, 3, 3, 3, 256], P(('dp', 'tm', 'rows'))
All inputs are finite; a program needn't handle non-finite values.
Results may differ from a plain program's by a relative error of at most 0.001.
Values may be sent and summed in bfloat16 or wider, within the bound.
A program may use at most 128 MiB of HBM per device.

v0:
```python
import jax
import jax.numpy as jnp
from jax import lax
from jax.sharding import PartitionSpec as P


def shift_from(shard, axis, by):
    peers = lax.axis_size(axis)
    pairs = [(i, i + by) for i in range(peers) if 0 <= i + by < peers]
    return lax.ppermute(shard, axis, pairs)


def pool_pairs(values, dim):
    n = values.shape[dim] // 2
    pad = [(0, 0)] * values.ndim
    pad[dim] = (1, 1)
    ext = jnp.pad(values, pad)
    shape = values.shape
    shifted = ext.reshape(shape[:dim] + (n + 1, 2) + shape[dim + 1 :]).sum(axis=dim + 1)
    aligned = values.reshape(shape[:dim] + (n, 2) + shape[dim + 1 :]).sum(axis=dim + 1)
    out = [
        lax.slice_in_dim(shifted, 1, n + 1, axis=dim),
        aligned,
        lax.slice_in_dim(shifted, 0, n, axis=dim),
    ]
    return jnp.stack(out, axis=dim + 1)


def with_halo(block, axis, dim, width):
    count = lax.axis_size(axis)
    forward = [(i, i + 1) for i in range(count - 1)]
    backward = [(target, source) for source, target in forward]
    low = lax.ppermute(
        lax.slice_in_dim(block, block.shape[dim] - width, None, axis=dim), axis, forward
    )
    high = lax.ppermute(lax.slice_in_dim(block, 0, width, axis=dim), axis, backward)
    return jnp.concatenate([low, block, high], axis=dim)


def body(latents, grad_out, kernel):
    frames = grad_out.shape[1]
    height = grad_out.shape[2]
    width = grad_out.shape[3]
    channels = latents.shape[4]
    outputs = grad_out.shape[4]
    devices = lax.axis_size("dp") * lax.axis_size("tm") * lax.axis_size("rows")
    factor = float(devices * frames * height * width) ** (-0.5)
    slab_count = lax.axis_size("rows")
    grad_whole = lax.all_gather(grad_out[0], "rows", axis=1, tiled=True)
    whole_height = grad_whole.shape[1]
    near = with_halo(grad_out[0], "rows", 1, 1)
    later = shift_from(near, "tm", -1)
    grad_all = jnp.concatenate([near, later], axis=0)
    grad_all = jnp.pad(grad_all, ((0, 0), (0, 0), (1, 1), (0, 0)))
    patches = []
    for a in range(3):
        for i in range(3):
            for j in range(3):
                patches.append(
                    grad_all[2 - a : 2 - a + frames, 2 - i : 2 - i + height, 2 - j : 2 - j + width]
                )
    patches = jnp.stack(patches, axis=3).reshape(frames * height * width, 27, outputs)
    grad_up = lax.dot_general(
        patches,
        kernel.reshape(27, channels, outputs),
        (((1, 2), (0, 2)), ((), ())),
        preferred_element_type=jnp.float32,
    )
    pooled = grad_up.reshape(frames, height // 2, 2, width // 2, 2, channels).sum(axis=(2, 4))
    grad_latents = pooled.astype(jnp.bfloat16)[None]
    groups = lax.axis_size("dp") * lax.axis_size("tm")
    share = channels // devices
    earlier = shift_from(latents, "tm", 1)
    with_earlier = jnp.concatenate([earlier, latents], axis=1)
    lead = with_earlier.shape[:4]
    regrouped = with_earlier.reshape(lead + (groups, slab_count, share))
    regrouped = jnp.swapaxes(regrouped, 4, 5).reshape(lead + (channels,))
    owned = lax.all_to_all(regrouped, "rows", split_axis=4, concat_axis=2, tiled=True)[0]
    group_channels = owned.shape[3]
    taps_a = jnp.stack([owned[a : a + frames] for a in range(3)], axis=0)
    pooled_grad = pool_pairs(pool_pairs(grad_whole.astype(jnp.float32), 1), 3)
    scaled = pooled_grad * 65537.0
    top = scaled - (scaled - pooled_grad)
    both = jnp.stack([top, pooled_grad - top], axis=0).astype(jnp.bfloat16)
    term = jnp.einsum("afrsc,xfrisjo->caijxo", taps_a, both, preferred_element_type=jnp.float32)
    term = (term[..., 0, :] + term[..., 1, :]) * factor
    term = term.reshape(group_channels, 3, 3, 3, outputs)
    term = lax.psum_scatter(term, "dp", scatter_dimension=0, tiled=True)
    weight_grad = lax.psum_scatter(term, "tm", scatter_dimension=0, tiled=True)
    return (grad_latents, weight_grad)


def solution(mesh):
    in_specs = (P("dp", "tm", "rows", None, None), P("dp", "tm", "rows", None, None), P())
    out_specs = (P("dp", "tm", "rows", None, None), P(("dp", "tm", "rows"), None, None, None, None))
    return jax.shard_map(body, mesh=mesh, in_specs=in_specs, out_specs=out_specs, check_vma=False)
```

profile of v0, /device:TPU:8, one launch (start us, length us, event | category | flops | bytes accessed | tf_op | source)
XLA Modules:
  0.0 247.5 jit_solution(9366353959574920145)
XLA Ops:
  7.2 3.4 %collective-permute-start.3 = (bf16[1,2,1,30,512]{4,1,3,2,0:T(2,128)(2,1)}, bf16[1,2,1,30,512]{4,1,3,2,0:T(2,128)(2,1)S(1)}, u32[]{:S(2)}, u32[]{:S(2)}) collective-permute-start(bf16[1,2,1,30,512]{4,1,3,2,0:T(2,128)(2,1)} %param.3), channel_id=1, source_target_pairs={{0,16},{16,32},{32,48},{1,17},{17,33},{33,49},{2,18},{18,34},{34,5... | collective-permute-start | bytes 184328 | tf_op jit(solution)/shard_map/ppermute | solution.py:10
  10.6 1.2 fusion.25
  11.8 4.2 %collective-permute-start = (bf16[2,1,60,256]{3,1,2,0:T(2,128)(2,1)S(1)}, bf16[2,1,60,256]{3,1,2,0:T(2,128)(2,1)S(1)}, u32[]{:S(2)}, u32[]{:S(2)}) collective-permute-start(bf16[2,1,60,256]{3,1,2,0:T(2,128)(2,1)S(1)} %get-tuple-element.46), channel_id=1, source_target_pairs={{0,1},{1,2},{2,3},{3,4},{4,5},{5,6},{6,7},{7,8},{8,9},{9,10},{10,1... | collective-permute-start | bytes 184328 | tf_op jit(solution)/shard_map/ppermute | solution.py:33
  16.0 1.3 collective-permute-start.1
  17.3 1.6 copy.102
  19.0 1.3 dynamic-slice
  20.9 1.0 pad_maximum_fusion.5
  23.0 1.6 reshape.353
  24.7 12.5 %all-to-all-start = ((bf16[16,2,1920]{2,1,0:T(2,128)(2,1)}), bf16[16,2,1920]{2,1,0:T(2,128)(2,1)S(1)}, u32[]{:S(2)}, u32[]{:S(2)}) async-start(bf16[16,2,1920]{2,1,0:T(2,128)(2,1)} %reshape.353), calls=%async_computation | async-start | bytes 245760 | tf_op jit(solution)/shard_map/all_to_all | solution.py:78
  37.7 1.7 collective-permute-start.2
  39.9 8.4 %all-to-all-done = bf16[16,2,1920]{2,1,0:T(2,128)(2,1)S(1)} async-done(((bf16[16,2,1920]{2,1,0:T(2,128)(2,1)}), bf16[16,2,1920]{2,1,0:T(2,128)(2,1)S(1)}, u32[]{:S(2)}, u32[]{:S(2)}) %all-to-all-start) | async-done | bytes 122912 | tf_op jit(solution)/shard_map/all_to_all | solution.py:78
  48.4 1.4 reshape.354
  49.8 0.9 slice_bitcast_fusion.2
  51.4 0.7 pad_slice_fusion
  52.1 0.7 copy_dynamic-update-slice_fusion.26
  53.1 0.7 copy_dynamic-update-slice_fusion.25
  53.8 0.7 copy_dynamic-update-slice_fusion.24
  54.4 0.7 copy_dynamic-update-slice_fusion.23
  55.1 0.7 copy_dynamic-update-slice_fusion.22
  55.8 0.7 copy_dynamic-update-slice_fusion.21
  56.5 0.7 copy_dynamic-update-slice_fusion.20
  57.2 0.7 copy_dynamic-update-slice_fusion.19
  57.8 0.7 copy_dynamic-update-slice_fusion.18
  58.5 0.7 copy_dynamic-update-slice_fusion.17
  59.2 1.6 pad_slice_fusion.1
  60.8 0.7 copy_dynamic-update-slice_fusion.16
  61.5 0.7 copy_dynamic-update-slice_fusion.15
  62.2 0.7 copy_dynamic-update-slice_fusion.14
  62.8 0.7 copy_dynamic-update-slice_fusion.13
  63.5 0.7 copy_dynamic-update-slice_fusion.12
  64.2 0.7 copy_dynamic-update-slice_fusion.11
  64.9 0.7 copy_dynamic-update-slice_fusion.10
  65.6 0.7 copy_dynamic-update-slice_fusion.9
  66.3 0.7 copy_dynamic-update-slice_fusion.8
  66.9 41.3 %all-gather.3.cloned.1.call-done = bf16[1,2,32,60,256]{4,1,3,0,2:T(2,128)(2,1)} async-done(((bf16[1,2,2,60,256]{4,1,3,0,2:T(2,128)(2,1)}), bf16[1,2,32,60,256]{4,1,3,0,2:T(2,128)(2,1)}) %all-gather.3.cloned.1.call-update) | async-done | bytes 1966096 | tf_op jit(solution)/shard_map/all_gather | solution.py:49
  108.2 2.9 %convert_bitcast_fusion = f32[2,32,60,256]{3,0,2,1:T(2,128)S(1)} fusion(bf16[1,2,32,60,256]{4,1,3,0,2:T(2,128)(2,1)} %all-gather.3.cloned.1.call-done), kind=kLoop, calls=%fused_computation.21 | loop fusion | flops 983040 | bytes 5898240 | tf_op jit(solution)/shard_map/convert_element_type | solution.py:81
  111.1 3.4 %pad.13 = f32[2,34,60,256]{3,0,2,1:T(2,128)} pad(f32[2,32,60,256]{3,0,2,1:T(2,128)S(1)} %convert_bitcast_fusion, f32[]{:T(128)} %constant.3.clone.1), padding=0_0x1_1x0_0x0_0 | pad | bytes 8110084 | tf_op jit(solution)/shard_map/jit(_pad)/pad | solution.py:17
  114.5 5.3 %reduce_sum.46 = f32[2,17,60,256]{3,0,2,1:T(2,128)S(1)} reduce(f32[2,17,2,60,256]{4,0,3,2,1:T(2,128)} %bitcast.115, f32[]{:T(128)} %constant.3.clone.1), dimensions={2}, to_apply=%region_1.2 | reduce | flops 522240 | bytes 6266884 | tf_op jit(solution)/shard_map/reduce_sum | solution.py:19
  119.8 16.3 %fusion.23 = (f32[2,16,60,256]{3,0,2,1:T(2,128)}, f32[2,16,1,60,256]{4,0,3,1,2:T(2,128)}, f32[2,16,1,60,256]{4,0,3,1,2:T(2,128)}, f32[2,16,60,256]{3,0,2,1:T(2,128)}) fusion(f32[2,17,60,256]{3,0,2,1:T(2,128)S(1)} %reduce_sum.46), kind=kLoop, calls=%fused_computation.89 | loop fusion | bytes 11796480 | tf_op jit(solution)/shard_map/slice | solution.py:22
  136.1 4.7 %reduce_sum.47 = f32[2,16,60,256]{3,0,2,1:T(2,128)S(1)} reduce(bf16[2,16,2,60,256]{4,0,3,2,1:T(2,128)(2,1)} %bitcast.117, f32[]{:T(128)} %constant.3.clone.1), dimensions={2}, to_apply=%region_2.3 | reduce | flops 491520 | bytes 3932164 | tf_op jit(solution)/shard_map/reduce_sum | solution.py:20
  140.9 1.9 copy.106
  142.7 1.0 copy-done.4
  143.7 5.5 %select_maximum_fusion = f32[2,16,3,62,256]{4,0,3,1,2:T(2,128)} fusion(f32[2,16,1,60,256]{4,0,3,1,2:T(2,128)S(1)} %copy-done.4, f32[2,16,1,60,256]{4,0,3,1,2:T(2,128)S(1)} %bitcast.114, f32[2,16,1,60,256]{4,0,3,1,2:T(2,128)S(1)} %copy-done.3), kind=kLoop, calls=%fused_computation.10 | loop fusion | flops 12189696 | bytes 11993088 | tf_op jit(solution)/shard_map/stack | solution.py:26
  149.2 7.7 %reduce.2 = f32[2,16,3,31,256]{4,0,3,1,2:T(2,128)S(1)} reduce(f32[2,16,3,31,2,256]{5,0,4,3,1,2:T(2,128)} %bitcast.113, f32[]{:T(128)} %constant.3.clone.1), dimensions={4}, to_apply=%region_3.4 | reduce | flops 761856 | bytes 9142276
  156.9 1.5 fusion.22
  159.1 0.9 copy-done
  160.7 0.9 maximum_reduce_fusion
  161.5 1.7 copy.159
  163.2 1.0 copy_bitcast_fusion
  164.2 2.2 fusion.1
  166.5 1.7 fusion.8
  168.3 1.1 fusion.16
  169.4 0.7 copy_dynamic-update-slice_fusion.7
  170.1 0.7 copy_dynamic-update-slice_fusion.6
  170.8 0.7 copy_dynamic-update-slice_fusion.5
  171.5 0.7 copy_dynamic-update-slice_fusion.4
  172.2 0.7 copy_dynamic-update-slice_fusion.3
  172.9 0.7 copy_dynamic-update-slice_fusion.2
  174.2 0.7 copy_dynamic-update-slice_fusion
  174.9 12.6 %reduce-scatter.3.cloned.1.call-done = f32[8,3,3,3,256]{4,0,1,3,2:T(8,128)} async-done(((f32[32,3,3,3,256]{4,0,1,3,2:T(8,128)}), f32[8,3,3,3,256]{4,0,1,3,2:T(8,128)}) %reduce-scatter.3.cloned.1.call-update) | async-done | bytes 221200 | tf_op jit(solution)/shard_map/reduce_scatter | solution.py:88
  187.6 6.1 %fusion.12 = bf16[2,30,512]{2,1,0:T(8,128)(2,1)S(1)} fusion(bf16[27,512,256,1,1,1]{2,1,0,5,4,3:T(8,128)(2,1)} %bitcast.158, bf16[2,1,2,30,2,27,256]{6,3,5,4,2,0,1:T(8,128)(2,1)} %copy_dynamic-update-slice_fusion), kind=kOutput, calls=%fused_computation.20 | convolution fusion | flops 1698785280 | bytes 10457088 | tf_op jit(solution)/shard_map/dot_general | solution.py:63
  193.7 0.7 copy.114
  194.4 44.7 %all-reduce.6.cloned.1.call-done = f32[8,3,3,3,256]{4,0,1,3,2:T(8,128)} async-done(((f32[8,3,3,3,256]{4,0,1,3,2:T(8,128)}), f32[8,3,3,3,256]{4,0,1,3,2:T(8,128)}) %all-reduce.6.cloned.1.call-update) | async-done | bytes 221200
  239.1 1.0 constant_dynamic-slice_fusion
  (47 shorter events, 5.9 us)
Async XLA Ops:
  7.2 30.1 %copy-start.5 = (bf16[1,2,2,60,256]{4,2,3,1,0:T(2,128)(2,1)S(1)}, bf16[1,2,2,60,256]{4,2,3,1,0:T(2,128)(2,1)}, u32[]{:S(2)}) copy-start(bf16[1,2,2,60,256]{4,2,3,1,0:T(2,128)(2,1)} %param.4) | copy-start | bytes 368644
  7.2 101.0 %all-gather.3.cloned.1.call-start = ((), (), s32[]{:S(2)}) async-start(), calls=%async_computation.3 | async-start | bytes 2088960 | tf_op jit(solution)/shard_map/all_gather | solution.py:49
  7.2 13.7 %collective-permute-start.3 = (bf16[1,2,1,30,512]{4,1,3,2,0:T(2,128)(2,1)}, bf16[1,2,1,30,512]{4,1,3,2,0:T(2,128)(2,1)S(1)}, u32[]{:S(2)}, u32[]{:S(2)}) collective-permute-start(bf16[1,2,1,30,512]{4,1,3,2,0:T(2,128)(2,1)} %param.3), channel_id=1, source_target_pairs={{0,16},{16,32},{32,48},{1,17},{17,33},{33,49},{2,18},{18,34},{34,5... | collective-permute-start | bytes 184328 | tf_op jit(solution)/shard_map/ppermute | solution.py:10
  11.8 25.4 %collective-permute-start = (bf16[2,1,60,256]{3,1,2,0:T(2,128)(2,1)S(1)}, bf16[2,1,60,256]{3,1,2,0:T(2,128)(2,1)S(1)}, u32[]{:S(2)}, u32[]{:S(2)}) collective-permute-start(bf16[2,1,60,256]{3,1,2,0:T(2,128)(2,1)S(1)} %get-tuple-element.46), channel_id=1, source_target_pairs={{0,1},{1,2},{2,3},{3,4},{4,5},{5,6},{6,7},{7,8},{8,9},{9,10},{10,1... | collective-permute-start | bytes 184328 | tf_op jit(solution)/shard_map/ppermute | solution.py:33
  16.0 21.2 %collective-permute-start.1 = (bf16[2,1,60,256]{3,1,2,0:T(2,128)(2,1)S(1)}, bf16[2,1,60,256]{3,1,2,0:T(2,128)(2,1)S(1)}, u32[]{:S(2)}, u32[]{:S(2)}) collective-permute-start(bf16[2,1,60,256]{3,1,2,0:T(2,128)(2,1)S(1)} %get-tuple-element.47), channel_id=1, source_target_pairs={{1,0},{2,1},{3,2},{4,3},{5,4},{6,5},{7,6},{8,7},{9,8},{10,9},{11,1... | collective-permute-start | bytes 184328 | tf_op jit(solution)/shard_map/ppermute | solution.py:36
  24.7 23.7 %all-to-all-start = ((bf16[16,2,1920]{2,1,0:T(2,128)(2,1)}), bf16[16,2,1920]{2,1,0:T(2,128)(2,1)S(1)}, u32[]{:S(2)}, u32[]{:S(2)}) async-start(bf16[16,2,1920]{2,1,0:T(2,128)(2,1)} %reshape.353), calls=%async_computation | async-start | bytes 245760 | tf_op jit(solution)/shard_map/all_to_all | solution.py:78
  37.2 150.3 %reduce-scatter.3.cloned.1.call-start = ((), (), s32[]{:S(2)}) async-start(), calls=%async_computation.2 | async-start | bytes 1105920 | tf_op jit(solution)/shard_map/reduce_scatter | solution.py:88
  37.7 13.0 %collective-permute-start.2 = (bf16[2,4,60,256]{3,1,2,0:T(4,128)(2,1)S(1)}, bf16[2,4,60,256]{3,1,2,0:T(4,128)(2,1)S(1)}, u32[]{:S(2)}, u32[]{:S(2)}) collective-permute-start(bf16[2,4,60,256]{3,1,2,0:T(4,128)(2,1)S(1)} %pad_maximum_fusion.2), channel_id=1, source_target_pairs={{16,0},{32,16},{48,32},{17,1},{33,17},{49,33},{18,2},{34,18},{50,3... | collective-permute-start | bytes 737288 | tf_op jit(solution)/shard_map/ppermute | solution.py:10
  140.8 1.9 copy-start.3
  140.8 2.8 %copy-start.4 = (f32[2,16,1,60,256]{4,0,3,1,2:T(2,128)S(1)}, f32[2,16,1,60,256]{4,0,3,1,2:T(2,128)}, u32[]{:S(2)}) copy-start(f32[2,16,1,60,256]{4,0,3,1,2:T(2,128)} %get-tuple-element.16) | copy-start | bytes 5898244
  156.9 1.6 copy-start.1
  158.5 1.5 copy-start
  158.5 2.2 copy-start.2
  164.2 2.3 copy-start.10
  164.2 2.3 copy-start.11
  164.2 2.3 copy-start.12
  168.2 1.9 copy-start.9
  168.2 2.5 %copy-start.8 = (bf16[2,2,60,256]{3,1,2,0:T(2,128)(2,1)S(1)}, bf16[2,2,60,256]{3,1,2,0:T(2,128)(2,1)}, u32[]{:S(2)}) copy-start(bf16[2,2,60,256]{3,1,2,0:T(2,128)(2,1)} %get-tuple-element.37) | copy-start | bytes 368644
  168.2 3.9 %copy-start.7 = (bf16[2,2,60,256]{3,1,2,0:T(2,128)(2,1)S(1)}, bf16[2,2,60,256]{3,1,2,0:T(2,128)(2,1)}, u32[]{:S(2)}) copy-start(bf16[2,2,60,256]{3,1,2,0:T(2,128)(2,1)} %get-tuple-element.38) | copy-start | bytes 368644
  168.3 4.6 %copy-start.6 = (bf16[2,2,60,256]{3,1,2,0:T(2,128)(2,1)S(1)}, bf16[2,2,60,256]{3,1,2,0:T(2,128)(2,1)}, u32[]{:S(2)}) copy-start(bf16[2,2,60,256]{3,1,2,0:T(2,128)(2,1)} %get-tuple-element.31) | copy-start | bytes 368644
  169.4 69.7 %all-reduce.6.cloned.1.call-start = ((), (), s32[]{:S(2)}) async-start(), calls=%async_computation.4 | async-start | bytes 442368
Sparse Core Ops, SparseCore 0:
  19.1 89.0 all-gather.2
  169.5 17.9 reduce-scatter.2
  189.9 49.1 all-reduce.5
where the time goes:
time: 251 us; the launch traced here: 247 us
  waiting for transfers between devices  107 us (43%)
  local copies, waits for them, and re-layouts  61.5 us (25%)
  other arithmetic  32.8 us (13%)
  starting transfers between devices  23.2 us (9%)
  between operations  15 us (6%)
  matrix products  7.87 us (3%)
    unnamed x4, waiting for transfers between devices  44.8 us
    all_gather x1, waiting for transfers between devices, body(): grad_whole = lax.all_gather(grad_out[0], 'rows', axis=1, tiled=True)  41.3 us
    unnamed x59, local copies, waits for them, and re-layouts  27.8 us
    slice x3, local copies, waits for them, and re-layouts, pool_pairs(): lax.slice_in_dim(shifted, 1, n + 1, axis=dim)  18.5 us
    reduce_scatter x1, waiting for transfers between devices, body(): term = lax.psum_scatter(term, 'dp', scatter_dimension=0, tiled=True)  12.6 us
    all_to_all x1, starting transfers between devices, body(): lax.all_to_all(regrouped, 'rows', split_axis=4, concat_axis=2, tiled=True)  12.5 us
    all_to_all x1, waiting for transfers between devices, body(): lax.all_to_all(regrouped, 'rows', split_axis=4, concat_axis=2, tiled=True)  8.43 us
    unnamed x1, other arithmetic  7.74 us
  transfers between devices with their start and end apart: 8, of which 4 were waited for; matrix products, arithmetic and copies ran while one was open for 16% of the time, Pallas kernels for 0%

commit v1 on v0

--- a/solution.py
+++ b/solution.py
@@ -46,7 +46,9 @@
     devices = lax.axis_size("dp") * lax.axis_size("tm") * lax.axis_size("rows")
     factor = float(devices * frames * height * width) ** (-0.5)
     slab_count = lax.axis_size("rows")
-    grad_whole = lax.all_gather(grad_out[0], "rows", axis=1, tiled=True)
+    block_2 = grad_out[0]
+    sent = jnp.stack([block_2] * lax.axis_size("rows"))
+    grad_whole = jnp.concatenate(lax.all_to_all(sent, "rows", 0, 0), axis=1)
     whole_height = grad_whole.shape[1]
     near = with_halo(grad_out[0], "rows", 1, 1)
     later = shift_from(near, "tm", -1)

time: 251 us -> 214 us (0.85); the launches traced: 247 us -> 214 us
  local copies, waits for them, and re-layouts: 61.5 us -> 46.5 us
  waiting for transfers between devices: 107 us -> 92.3 us
  other arithmetic: 32.8 us -> 25.1 us
  starting transfers between devices: 23.2 us -> 26.8 us
    all_gather x1 -> x0, waiting for transfers between devices: 41.3 us -> none  [body(): grad_whole = lax.all_gather(grad_out[0], 'rows', axis=1, tiled=True)]
    all_to_all x0 -> x1, waiting for transfers between devices: none -> 28.6 us  [body(): grad_whole = jnp.concatenate(lax.all_to_all(sent, 'rows', 0, 0), axis=1)]
    slice x3, local copies, waits for them, and re-layouts: 18.5 us -> 5.57 us  [pool_pairs(): lax.slice_in_dim(shifted, 1, n + 1, axis=dim)]
    all_to_all x0 -> x1, starting transfers between devices: none -> 3.72 us  [body(): grad_whole = jnp.concatenate(lax.all_to_all(sent, 'rows', 0, 0), axis=1)]
    convert_element_type x1 -> x0, other arithmetic: 2.89 us -> none  [body(): pooled_grad = pool_pairs(pool_pairs(grad_whole.astype(jnp.float32), 1), 3)]
    reduce_sum x1, other arithmetic: 5.32 us -> 2.51 us  [pool_pairs(): ext.reshape(shape[:dim] + (n + 1, 2) + shape[dim + 1:]).sum(axis=dim + 1)]
    unnamed x59 -> x56, local copies, waits for them, and re-layouts: 27.8 us -> 25.2 us
    unnamed x4 -> x3, waiting for transfers between devices: 44.8 us -> 44.8 us
  transfers between devices with their start and end apart: 8 -> 8, of which waited for: 4 -> 4; matrix products, arithmetic and copies ran while one was open for 16% -> 20% of each run, Pallas kernels for 0% -> 0%
where the time goes in v1:
time: 214 us
  waiting for transfers between devices  92.3 us (43%)
  local copies, waits for them, and re-layouts  46.5 us (22%)
  starting transfers between devices  26.8 us (13%)
  other arithmetic  25.1 us (12%)
  between operations  15.1 us (7%)
  matrix products  7.87 us (4%)
    unnamed x3, waiting for transfers between devices  44.8 us
    all_to_all x1, waiting for transfers between devices, body(): grad_whole = jnp.concatenate(lax.all_to_all(sent, 'rows', 0, 0), axis=1)  28.6 us
    unnamed x56, local copies, waits for them, and re-layouts  25.2 us
    all_to_all x1, starting transfers between devices, body(): lax.all_to_all(regrouped, 'rows', split_axis=4, concat_axis=2, tiled=True)  12.5 us
    reduce_scatter x1, waiting for transfers between devices, body(): term = lax.psum_scatter(term, 'dp', scatter_dimension=0, tiled=True)  10.8 us
    all_to_all x1, waiting for transfers between devices, body(): lax.all_to_all(regrouped, 'rows', split_axis=4, concat_axis=2, tiled=True)  8.1 us
    unnamed x1, other arithmetic  7.74 us
    dot_general x1, matrix products, body(): lax.dot_general(patches, kernel.reshape(27, channels, outputs), (((1, 2),...  6.12 us
  transfers between devices with their start and end apart: 8, of which 4 were waited for; matrix products, arithmetic and copies ran while one was open for 20% of the time, Pallas kernels for 0%

profile of v1, /device:TPU:8, one launch (start us, length us, event | category | flops | bytes accessed | tf_op | source)
XLA Modules:
  0.0 213.7 jit_solution(15756712796282381123)
XLA Ops:
  7.2 3.5 %collective-permute-start.3 = (bf16[1,2,1,30,512]{4,1,3,2,0:T(2,128)(2,1)}, bf16[1,2,1,30,512]{4,1,3,2,0:T(2,128)(2,1)S(1)}, u32[]{:S(2)}, u32[]{:S(2)}) collective-permute-start(bf16[1,2,1,30,512]{4,1,3,2,0:T(2,128)(2,1)} %param.3), channel_id=1, source_target_pairs={{0,16},{16,32},{32,48},{1,17},{17,33},{33,49},{2,18},{18,34},{34,5... | collective-permute-start | bytes 184328 | tf_op jit(solution)/shard_map/ppermute | solution.py:10
  10.7 1.2 fusion.25
  11.9 4.2 %collective-permute-start = (bf16[2,1,60,256]{3,1,2,0:T(2,128)(2,1)S(1)}, bf16[2,1,60,256]{3,1,2,0:T(2,128)(2,1)S(1)}, u32[]{:S(2)}, u32[]{:S(2)}) collective-permute-start(bf16[2,1,60,256]{3,1,2,0:T(2,128)(2,1)S(1)} %get-tuple-element.46), channel_id=1, source_target_pairs={{0,1},{1,2},{2,3},{3,4},{4,5},{5,6},{6,7},{7,8},{8,9},{9,10},{10,1... | collective-permute-start | bytes 184328 | tf_op jit(solution)/shard_map/ppermute | solution.py:33
  16.1 1.3 collective-permute-start.1
  17.4 1.0 copy.103
  18.4 1.3 dynamic-slice
  20.4 1.0 pad_maximum_fusion.5
  22.5 1.7 reshape.358
  24.1 12.5 %all-to-all-start.1 = ((bf16[16,2,1920]{2,1,0:T(2,128)(2,1)}), bf16[16,2,1920]{2,1,0:T(2,128)(2,1)S(1)}, u32[]{:S(2)}, u32[]{:S(2)}) async-start(bf16[16,2,1920]{2,1,0:T(2,128)(2,1)} %reshape.358), calls=%async_computation.1 | async-start | bytes 245760 | tf_op jit(solution)/shard_map/all_to_all | solution.py:80
  36.7 1.1 pad_maximum_fusion.2
  37.8 1.3 collective-permute-start.2
  39.6 8.1 %all-to-all-done.1 = bf16[16,2,1920]{2,1,0:T(2,128)(2,1)S(1)} async-done(((bf16[16,2,1920]{2,1,0:T(2,128)(2,1)}), bf16[16,2,1920]{2,1,0:T(2,128)(2,1)S(1)}, u32[]{:S(2)}, u32[]{:S(2)}) %all-to-all-start.1) | async-done | bytes 122912 | tf_op jit(solution)/shard_map/all_to_all | solution.py:80
  47.7 2.3 %stack.165 = bf16[16,2,2,60,256]{4,1,3,2,0:T(2,128)(2,1)} broadcast(bf16[2,2,60,256]{3,0,2,1:T(2,128)(2,1)S(1)} %copy.103), dimensions={1,2,3,4} | broadcast | bytes 2088960 | tf_op jit(solution)/shard_map/stack | solution.py:50
  50.1 3.7 %all-to-all-start = ((bf16[16,2,2,60,256]{4,1,3,2,0:T(2,128)(2,1)}), bf16[16,2,2,60,256]{4,1,3,2,0:T(2,128)(2,1)S(1)}, u32[]{:S(2)}, u32[]{:S(2)}) async-start(bf16[16,2,2,60,256]{4,1,3,2,0:T(2,128)(2,1)} %stack.165), calls=%async_computation | async-start | bytes 3932160 | tf_op jit(solution)/shard_map/all_to_all | solution.py:51
  54.0 1.4 reshape.359
  55.5 0.9 slice_bitcast_fusion.2
  57.1 0.7 pad_slice_fusion
  57.8 0.7 copy_dynamic-update-slice_fusion.26
  58.7 0.7 copy_dynamic-update-slice_fusion.25
  59.4 0.7 copy_dynamic-update-slice_fusion.24
  60.1 0.7 copy_dynamic-update-slice_fusion.23
  60.8 0.7 copy_dynamic-update-slice_fusion.22
  61.4 0.7 copy_dynamic-update-slice_fusion.21
  62.1 0.7 copy_dynamic-update-slice_fusion.20
  62.8 0.7 copy_dynamic-update-slice_fusion.19
  63.5 0.7 copy_dynamic-update-slice_fusion.18
  64.2 0.7 copy_dynamic-update-slice_fusion.17
  64.8 1.6 pad_slice_fusion.1
  66.4 0.7 copy_dynamic-update-slice_fusion.16
  67.1 0.7 copy_dynamic-update-slice_fusion.15
  67.8 0.7 copy_dynamic-update-slice_fusion.14
  68.5 0.7 copy_dynamic-update-slice_fusion.13
  69.2 0.7 copy_dynamic-update-slice_fusion.12
  69.8 0.7 copy_dynamic-update-slice_fusion.11
  71.2 0.7 copy_dynamic-update-slice_fusion.9
  71.9 0.7 copy_dynamic-update-slice_fusion.8
  72.6 28.6 %all-to-all-done = bf16[16,2,2,60,256]{4,1,3,2,0:T(2,128)(2,1)S(1)} async-done(((bf16[16,2,2,60,256]{4,1,3,2,0:T(2,128)(2,1)}), bf16[16,2,2,60,256]{4,1,3,2,0:T(2,128)(2,1)S(1)}, u32[]{:S(2)}, u32[]{:S(2)}) %all-to-all-start) | async-done | bytes 1966112 | tf_op jit(solution)/shard_map/all_to_all | solution.py:51
  101.2 1.6 pad.14
  102.8 2.5 %convert_reduce_fusion = f32[2,17,60,256]{3,0,2,1:T(2,128)S(1)} fusion(bf16[2,17,2,60,256]{4,0,3,2,1:T(2,128)(2,1)S(1)} %bitcast.120), kind=kLoop, calls=%fused_computation.13 | loop fusion | flops 1566720 | bytes 4177920 | tf_op jit(solution)/shard_map/reduce_sum | solution.py:19
  105.3 3.4 %fusion.23 = (f32[2,16,60,256]{3,0,2,1:T(2,128)}, f32[2,16,1,60,256]{4,0,3,1,2:T(2,128)S(1)}, f32[2,16,1,60,256]{4,0,3,1,2:T(2,128)S(1)}, f32[2,16,60,256]{3,0,2,1:T(2,128)}) fusion(f32[2,17,60,256]{3,0,2,1:T(2,128)S(1)} %convert_reduce_fusion), kind=kLoop, calls=%fused_computation.90 | loop fusion | bytes 11796480 | tf_op jit(solution)/shard_map/slice | solution.py:22
  108.7 2.4 %convert_reduce_fusion.1 = f32[16,2,60,256]{3,1,2,0:T(2,128)S(1)} fusion(bf16[16,2,2,60,256]{4,1,3,2,0:T(2,128)(2,1)S(1)} %all-to-all-done), kind=kLoop, calls=%fused_computation.14 | loop fusion | flops 1474560 | bytes 3932160 | tf_op jit(solution)/shard_map/reduce_sum | solution.py:20
  111.1 5.5 %select_maximum_fusion = f32[2,16,3,62,256]{4,0,3,1,2:T(2,128)} fusion(f32[2,16,1,60,256]{4,0,3,1,2:T(2,128)S(1)} %get-tuple-element.16, f32[2,16,1,60,256]{4,0,3,1,2:T(2,128)S(1)} %bitcast.117, f32[2,16,1,60,256]{4,0,3,1,2:T(2,128)S(1)} %get-tuple-element.15), kind=kLoop, calls=%fused_computation.10 | loop fusion | flops 12189696 | bytes 11993088 | tf_op jit(solution)/shard_map/stack | solution.py:26
  116.6 7.7 %reduce.3 = f32[2,16,3,31,256]{4,0,3,1,2:T(2,128)S(1)} reduce(f32[2,16,3,31,2,256]{5,0,4,3,1,2:T(2,128)} %bitcast.115, f32[]{:T(128)} %constant.8.clone.1), dimensions={4}, to_apply=%region_3.4 | reduce | flops 761856 | bytes 9142276
  124.4 1.5 fusion.22
  126.6 0.9 copy-done.2
  128.8 0.8 maximum_reduce_fusion
  129.6 1.7 copy.160
  131.3 1.2 copy_bitcast_fusion
  132.5 1.9 fusion.1
  134.5 1.8 fusion.8
  136.3 1.1 fusion.16
  137.4 0.7 copy_dynamic-update-slice_fusion.7
  138.1 0.7 copy_dynamic-update-slice_fusion.6
  138.8 0.7 copy_dynamic-update-slice_fusion.5
  139.4 0.7 copy_dynamic-update-slice_fusion.4
  140.1 0.7 copy_dynamic-update-slice_fusion.3
  140.8 0.7 copy_dynamic-update-slice_fusion.2
  141.5 0.7 copy_dynamic-update-slice_fusion.1
  142.2 0.7 copy_dynamic-update-slice_fusion
  142.9 10.8 %reduce-scatter.3.cloned.1.call-done = f32[8,3,3,3,256]{4,0,1,3,2:T(8,128)} async-done(((f32[32,3,3,3,256]{4,0,1,3,2:T(8,128)}), f32[8,3,3,3,256]{4,0,1,3,2:T(8,128)}) %reduce-scatter.3.cloned.1.call-update) | async-done | bytes 221200 | tf_op jit(solution)/shard_map/reduce_scatter | solution.py:90
  153.7 6.1 %fusion.12 = bf16[2,30,512]{2,1,0:T(8,128)(2,1)S(1)} fusion(bf16[27,512,256,1,1,1]{2,1,0,5,4,3:T(8,128)(2,1)} %bitcast.162, bf16[2,1,2,30,2,27,256]{6,3,5,4,2,0,1:T(8,128)(2,1)} %copy_dynamic-update-slice_fusion), kind=kOutput, calls=%fused_computation.22 | convolution fusion | flops 1698785280 | bytes 10457088 | tf_op jit(solution)/shard_map/dot_general | solution.py:65
  159.9 0.7 copy.115
  160.6 44.7 %all-reduce.6.cloned.1.call-done = f32[8,3,3,3,256]{4,0,1,3,2:T(8,128)} async-done(((f32[8,3,3,3,256]{4,0,1,3,2:T(8,128)}), f32[8,3,3,3,256]{4,0,1,3,2:T(8,128)}) %all-reduce.6.cloned.1.call-update) | async-done | bytes 221200
  205.3 1.0 constant_dynamic-slice_fusion
  (44 shorter events, 6.2 us)
Async XLA Ops:
  7.2 29.5 %copy-start.4 = (bf16[1,2,2,60,256]{4,2,3,1,0:T(2,128)(2,1)S(1)}, bf16[1,2,2,60,256]{4,2,3,1,0:T(2,128)(2,1)}, u32[]{:S(2)}) copy-start(bf16[1,2,2,60,256]{4,2,3,1,0:T(2,128)(2,1)} %param.4) | copy-start | bytes 368644
  7.2 13.2 %collective-permute-start.3 = (bf16[1,2,1,30,512]{4,1,3,2,0:T(2,128)(2,1)}, bf16[1,2,1,30,512]{4,1,3,2,0:T(2,128)(2,1)S(1)}, u32[]{:S(2)}, u32[]{:S(2)}) collective-permute-start(bf16[1,2,1,30,512]{4,1,3,2,0:T(2,128)(2,1)} %param.3), channel_id=1, source_target_pairs={{0,16},{16,32},{32,48},{1,17},{17,33},{33,49},{2,18},{18,34},{34,5... | collective-permute-start | bytes 184328 | tf_op jit(solution)/shard_map/ppermute | solution.py:10
  11.9 24.8 %collective-permute-start = (bf16[2,1,60,256]{3,1,2,0:T(2,128)(2,1)S(1)}, bf16[2,1,60,256]{3,1,2,0:T(2,128)(2,1)S(1)}, u32[]{:S(2)}, u32[]{:S(2)}) collective-permute-start(bf16[2,1,60,256]{3,1,2,0:T(2,128)(2,1)S(1)} %get-tuple-element.46), channel_id=1, source_target_pairs={{0,1},{1,2},{2,3},{3,4},{4,5},{5,6},{6,7},{7,8},{8,9},{9,10},{10,1... | collective-permute-start | bytes 184328 | tf_op jit(solution)/shard_map/ppermute | solution.py:33
  16.1 20.6 %collective-permute-start.1 = (bf16[2,1,60,256]{3,1,2,0:T(2,128)(2,1)S(1)}, bf16[2,1,60,256]{3,1,2,0:T(2,128)(2,1)S(1)}, u32[]{:S(2)}, u32[]{:S(2)}) collective-permute-start(bf16[2,1,60,256]{3,1,2,0:T(2,128)(2,1)S(1)} %get-tuple-element.47), channel_id=1, source_target_pairs={{1,0},{2,1},{3,2},{4,3},{5,4},{6,5},{7,6},{8,7},{9,8},{10,9},{11,1... | collective-permute-start | bytes 184328 | tf_op jit(solution)/shard_map/ppermute | solution.py:36
  24.1 23.6 %all-to-all-start.1 = ((bf16[16,2,1920]{2,1,0:T(2,128)(2,1)}), bf16[16,2,1920]{2,1,0:T(2,128)(2,1)S(1)}, u32[]{:S(2)}, u32[]{:S(2)}) async-start(bf16[16,2,1920]{2,1,0:T(2,128)(2,1)} %reshape.358), calls=%async_computation.1 | async-start | bytes 245760 | tf_op jit(solution)/shard_map/all_to_all | solution.py:80
  37.8 18.6 %collective-permute-start.2 = (bf16[2,4,60,256]{3,1,2,0:T(4,128)(2,1)}, bf16[2,4,60,256]{3,1,2,0:T(4,128)(2,1)S(1)}, u32[]{:S(2)}, u32[]{:S(2)}) collective-permute-start(bf16[2,4,60,256]{3,1,2,0:T(4,128)(2,1)} %pad_maximum_fusion.2), channel_id=1, source_target_pairs={{16,0},{32,16},{48,32},{17,1},{33,17},{49,33},{18,2},{34,18},{50,3... | collective-permute-start | bytes 737288 | tf_op jit(solution)/shard_map/ppermute | solution.py:10
  50.1 51.1 %all-to-all-start = ((bf16[16,2,2,60,256]{4,1,3,2,0:T(2,128)(2,1)}), bf16[16,2,2,60,256]{4,1,3,2,0:T(2,128)(2,1)S(1)}, u32[]{:S(2)}, u32[]{:S(2)}) async-start(bf16[16,2,2,60,256]{4,1,3,2,0:T(2,128)(2,1)} %stack.165), calls=%async_computation | async-start | bytes 3932160 | tf_op jit(solution)/shard_map/all_to_all | solution.py:51
  53.8 99.9 %reduce-scatter.3.cloned.1.call-start = ((), (), s32[]{:S(2)}) async-start(), calls=%async_computation.3 | async-start | bytes 1105920 | tf_op jit(solution)/shard_map/reduce_scatter | solution.py:90
  111.1 5.5 %copy-start = (f32[16,2,60,256]{3,1,2,0:T(2,128)}, f32[16,2,60,256]{3,1,2,0:T(2,128)S(1)}, u32[]{:S(2)}) copy-start(f32[16,2,60,256]{3,1,2,0:T(2,128)S(1)} %convert_reduce_fusion.1) | copy-start | bytes 5898244
  124.4 1.6 copy-start.3
  125.9 1.5 copy-start.2
  125.9 2.2 %copy-start.1 = (f32[16,2,60,256]{3,1,2,0:T(2,128)S(1)}, f32[16,2,60,256]{3,1,2,0:T(2,128)}, u32[]{:S(2)}) copy-start(f32[16,2,60,256]{3,1,2,0:T(2,128)} %copy-done) | copy-start | bytes 5898244
  132.5 1.9 copy-start.9
  132.5 1.9 copy-start.10
  132.5 1.9 copy-start.11
  136.2 1.9 copy-start.8
  136.2 2.5 %copy-start.7 = (bf16[2,2,60,256]{3,1,2,0:T(2,128)(2,1)S(1)}, bf16[2,2,60,256]{3,1,2,0:T(2,128)(2,1)}, u32[]{:S(2)}) copy-start(bf16[2,2,60,256]{3,1,2,0:T(2,128)(2,1)} %get-tuple-element.37) | copy-start | bytes 368644
  136.2 3.9 %copy-start.6 = (bf16[2,2,60,256]{3,1,2,0:T(2,128)(2,1)S(1)}, bf16[2,2,60,256]{3,1,2,0:T(2,128)(2,1)}, u32[]{:S(2)}) copy-start(bf16[2,2,60,256]{3,1,2,0:T(2,128)(2,1)} %get-tuple-element.38) | copy-start | bytes 368644
  136.2 4.6 %copy-start.5 = (bf16[2,2,60,256]{3,1,2,0:T(2,128)(2,1)S(1)}, bf16[2,2,60,256]{3,1,2,0:T(2,128)(2,1)}, u32[]{:S(2)}) copy-start(bf16[2,2,60,256]{3,1,2,0:T(2,128)(2,1)} %get-tuple-element.31) | copy-start | bytes 368644
  137.4 67.9 %all-reduce.6.cloned.1.call-start = ((), (), s32[]{:S(2)}) async-start(), calls=%async_computation.4 | async-start | bytes 442368
Sparse Core Ops, SparseCore 0:
  137.5 16.1 reduce-scatter.2
  156.1 49.1 all-reduce.5
